TPU v7x, 128 devices: a whole 4x4x4 slice. The times are simulated.
128 devices in a mesh: row: 4 (over z_hi, core), col: 32 (over x, z_lo, y).
Axes of the slice: x: 4, y: 4, z: 4 (z_hi: 2, z_lo: 2; z = z_hi * 2 + z_lo), core: 2. Of those that a mesh axis runs over, the one named last changes fastest.
Arguments:
- right_side: float32 [131072, 128], P(('row', 'col')), may hold values from -150 to 150
- block_values: bfloat16 [64, 917504], P(None, ('row', 'col')), may hold values from -1 to 2, as said below
- block_cols: int32 [14336], P(('row', 'col')), may hold values from 0 to 511, as said below
- row_ptrs: int32 [8320], P(('row', 'col')), may hold values from 0 to 112, as said below
- precond: float32 [131072, 1024], P(('row', 'col')), may hold values from -1 to 2, as said below
Outputs:
- solution: float32 [131072, 128], P(('row', 'col'))
- residual: float32 [131072, 128], P(('row', 'col'))
Inputs may be any that keep to these rules, and one draw needn't show every extreme that they name: `row_ptrs`: in each tile t the 65 pointers from index t * (65) on never fall, start at 0 and end at 112. `block_cols`: each of the 2048 block rows of A holds 7 blocks. `block_values`: with the pattern, the blocks form a symmetric matrix A. `precond`: each 1024 x 1024 block is lower triangular with a positive diagonal.
All inputs are finite; a program needn't handle non-finite values.
Results may differ from a plain program's by a relative error of at most 0.0076.
Values may be sent and summed in bfloat16 or wider, within the bound.
A program may use at most 128 MiB of HBM per device.

v0:
```python
import jax
import jax.numpy as jnp
from jax import lax
from jax.sharding import PartitionSpec as P

ITERS = 2


def per_device(right_side, block_values, block_cols, row_ptrs, precond):
    block_size = block_values.shape[0]
    slot_count = block_cols.shape[0]
    tile_rows = row_ptrs.shape[0] - 1
    seg_rows = right_side.shape[0]
    rhs_count = right_side.shape[1]
    tile_cols = lax.axis_size("col") * (seg_rows // block_size)
    tile_blocks = block_values.reshape(block_size, slot_count, block_size)
    slot_index = jnp.arange(slot_count, dtype=jnp.int32)
    slot_rows = jnp.sum((slot_index[:, None] >= row_ptrs[None, 1:]).astype(jnp.int32), axis=1)
    solution = jnp.zeros_like(right_side)
    residual = right_side
    direction = right_side
    image_vec = right_side
    alpha_prev = jnp.ones((rhs_count,), jnp.float32)
    gamma_prev = jnp.ones((rhs_count,), jnp.float32)
    for iteration in range(ITERS):
        half_step = jnp.dot(
            precond, residual, precision=lax.Precision.HIGHEST, preferred_element_type=jnp.float32
        )
        smoothed = lax.dot_general(
            precond,
            half_step,
            (((0,), (0,)), ((), ())),
            precision=lax.Precision.HIGHEST,
            preferred_element_type=jnp.float32,
        )
        local_energy = jnp.sum(residual * smoothed, axis=0)
        gamma_now = lax.psum(local_energy, ("row", "col"))
        gathered = lax.all_gather(smoothed.astype(jnp.bfloat16), "col", axis=0, tiled=True)
        pieces = gathered.reshape(tile_cols, block_size, rhs_count)[block_cols]
        products = jnp.einsum(
            "ibj,bjk->bik", tile_blocks, pieces, preferred_element_type=jnp.float32
        )
        partial_value = jax.ops.segment_sum(
            products, slot_rows, num_segments=tile_rows, indices_are_sorted=True
        )
        applied = lax.psum_scatter(
            partial_value.reshape(tile_rows * block_size, rhs_count),
            "row",
            scatter_dimension=0,
            tiled=True,
        )
        delta_now = lax.psum(jnp.sum(smoothed * applied, axis=0), ("row", "col"))
        if iteration == 0:
            alpha_now = gamma_now / delta_now
            direction = smoothed
            image_vec = applied
        else:
            beta_now = gamma_now / gamma_prev
            alpha_now = gamma_now / (delta_now - beta_now * gamma_now / alpha_prev)
            direction = smoothed + beta_now * direction
            image_vec = applied + beta_now * image_vec
        solution = solution + alpha_now * direction
        residual = residual - alpha_now * image_vec
        gamma_prev = gamma_now
        alpha_prev = alpha_now
    return (solution, residual)


def solution(mesh):
    return jax.shard_map(
        per_device,
        mesh=mesh,
        in_specs=(
            P(("row", "col"), None),
            P(None, ("row", "col")),
            P(("row", "col")),
            P(("row", "col")),
            P(("row", "col"), None),
        ),
        out_specs=(P(("row", "col"), None), P(("row", "col"), None)),
        check_vma=False,
    )
```

profile of v0, /device:TPU:1, one launch (start us, length us, event | category | flops | bytes accessed | tf_op | source)
XLA Modules:
  0.0 653.4 jit_solution(4864520073481413777)
XLA Ops:
  7.2 0.0 all-gather.3.cloned.1.call-start
  7.2 0.0 copy-start
  7.2 5.4 fusion.5
  12.7 0.0 copy-done
  12.7 0.0 copy-start.7
  12.7 3.2 fusion.3
  15.9 0.0 all-gather.3.cloned.1.call-update
  15.9 0.0 reduce-scatter.3.cloned.1.call-start
  16.0 0.0 copy-done.7
  16.0 0.1 slice.3
  16.0 2.3 reshape.24
  18.3 0.0 copy-done.8
  18.3 0.0 copy-start.2
  18.4 0.1 convert_reduce_fusion
  18.5 148.9 %all-gather.3.cloned.1.call-done = bf16[32768,128]{0,1:T(8,128)(2,1)} async-done(((bf16[1024,128]{0,1:T(8,128)(2,1)}), bf16[32768,128]{0,1:T(8,128)(2,1)}) %all-gather.3.cloned.1.call-update) | async-done | bytes 8388624 | tf_op jit(solution)/shard_map/all_gather | solution.py:38
  167.4 11.9 %copy.26 = bf16[32768,128]{1,0:T(8,128)(2,1)} copy(bf16[32768,128]{0,1:T(8,128)(2,1)} %all-gather.3.cloned.1.call-done) | data formatting | bytes 16777216 | tf_op jit(solution)/shard_map/all_gather | solution.py:38
  179.3 5.4 gather_fusion
  184.7 0.0 copy-done.2
  184.7 3.9 convolution_bitcast_fusion.1
  188.6 0.2 broadcast.13.clone
  188.9 11.9 %scatter_fusion = f32[64,64,128]{2,1,0:T(8,128)S(1)} fusion(f32[64,64,128]{2,1,0:T(8,128)S(1)} %broadcast.13.clone, s32[112]{0:T(128)S(1)} %convert_reduce_fusion, f32[112,64,128]{2,1,0:T(8,128)} %convolution_bitcast_fusion.1), kind=kCustom, calls=%fused_computation.2 | custom fusion | flops 917504 | bytes 11010496 | tf_op jit(solution)/shard_map/scatter-add | solution.py:43
  200.8 1.9 copy.28
  202.7 0.0 reduce-scatter.3.cloned.1.call-update
  202.7 0.0 all-gather.5.cloned.1.call-start
  202.7 1.0 copy-done.6
  203.7 0.2 copy.25
  203.9 57.5 %reduce-scatter.3.cloned.1.call-done = f32[1024,128]{0,1:T(8,128)} async-done(((f32[4096,128]{0,1:T(8,128)}), f32[1024,128]{0,1:T(8,128)}) %reduce-scatter.3.cloned.1.call-update) | async-done | bytes 524304 | tf_op jit(solution)/shard_map/reduce_scatter | solution.py:46
  261.4 1.2 multiply_reduce_fusion.2
  262.6 64.9 %all-reduce.1 = (f32[128]{0:T(128)S(1)}, f32[128]{0:T(128)S(1)}) all-reduce(f32[128]{0:T(128)S(1)} %get-tuple-element.11, f32[128]{0:T(128)S(1)} %get-tuple-element.10), channel_id=1, replica_groups=mesh['row'=4,'col'=32] {'row','col'}, use_global_device_ids=true, to_apply=%region_1.0 | all-reduce | flops 256 | bytes 2048 | tf_op jit(solution)/shard_map/psum | solution.py:37
  327.5 6.9 %fusion.2 = f32[128,1024]{1,0:T(8,128)S(1)} fusion(f32[1024,1024]{1,0:T(8,128)} %param.9, f32[1024,128]{0,1:T(8,128)S(1)} %copy.25, f32[1024,128]{0,1:T(8,128)} %reduce-scatter.3.cloned.1.call-done, f32[128]{0:T(128)S(1)} %div.12), kind=kOutput, calls=%fused_computation.22 | convolution fusion | flops 1610874880 | bytes 5767680 | tf_op jit(solution)/shard_map/dot_general | solution.py:26
  334.5 0.0 copy-done.1
  334.5 3.3 fusion.4
  337.8 0.0 all-gather.5.cloned.1.call-update
  337.8 0.0 reduce-scatter.5.cloned.1.call-start
  337.8 145.3 %all-gather.5.cloned.1.call-done = bf16[32768,128]{0,1:T(8,128)(2,1)} async-done(((bf16[1024,128]{0,1:T(8,128)(2,1)}), bf16[32768,128]{0,1:T(8,128)(2,1)}) %all-gather.5.cloned.1.call-update) | async-done | bytes 8388624 | tf_op jit(solution)/shard_map/all_gather | solution.py:38
  483.2 11.9 %copy.30 = bf16[32768,128]{1,0:T(8,128)(2,1)} copy(bf16[32768,128]{0,1:T(8,128)(2,1)} %all-gather.5.cloned.1.call-done) | data formatting | bytes 16777216 | tf_op jit(solution)/shard_map/all_gather | solution.py:38
  495.1 5.6 gather_fusion.1
  500.7 3.9 convolution_bitcast_fusion
  504.7 0.2 broadcast.13
  504.9 11.9 %scatter_fusion.1 = f32[64,64,128]{2,1,0:T(8,128)S(1)} fusion(f32[64,64,128]{2,1,0:T(8,128)S(1)} %broadcast.13, s32[112]{0:T(128)S(1)} %convert_reduce_fusion, f32[112,64,128]{2,1,0:T(8,128)} %convolution_bitcast_fusion), kind=kCustom, calls=%fused_computation.3 | custom fusion | flops 917504 | bytes 11010496 | tf_op jit(solution)/shard_map/scatter-add | solution.py:43
  516.8 1.9 copy.32
  518.7 0.0 reduce-scatter.5.cloned.1.call-update
  518.7 58.8 %reduce-scatter.5.cloned.1.call-done = f32[1024,128]{0,1:T(8,128)} async-done(((f32[4096,128]{0,1:T(8,128)}), f32[1024,128]{0,1:T(8,128)}) %reduce-scatter.5.cloned.1.call-update) | async-done | bytes 524304 | tf_op jit(solution)/shard_map/reduce_scatter | solution.py:46
  577.5 1.3 multiply_reduce_fusion
  578.7 64.7 %all-reduce = (f32[128]{0:T(128)S(1)}, f32[128]{0:T(128)S(1)}) all-reduce(f32[128]{0:T(128)S(1)} %get-tuple-element.9, f32[128]{0:T(128)S(1)} %get-tuple-element.8), channel_id=1, replica_groups=mesh['row'=4,'col'=32] {'row','col'}, use_global_device_ids=true, to_apply=%region_8.0 | all-reduce | flops 256 | bytes 2048 | tf_op jit(solution)/shard_map/psum | solution.py:37
  643.5 1.4 multiply_subtract_fusion
  644.9 1.0 copy.34
  645.9 1.0 copy.33
  (13 shorter events, 0.0 us)
Async XLA Ops:
  7.2 160.2 %all-gather.3.cloned.1.call-start = ((), (), s32[]{:S(2)}) async-start(), calls=%async_computation.2 | async-start | bytes 8650752 | tf_op jit(solution)/shard_map/all_gather | solution.py:38
  7.2 5.5 copy-start
  12.7 3.3 copy-start.7
  15.9 2.4 copy-start.8
  15.9 245.5 %reduce-scatter.3.cloned.1.call-start = ((), (), s32[]{:S(2)}) async-start(), calls=%async_computation.3 | async-start | bytes 2621440 | tf_op jit(solution)/shard_map/reduce_scatter | solution.py:46
  18.3 166.4 %copy-start.2 = (bf16[64,112,64]{2,1,0:T(8,128)(2,1)}, bf16[64,112,64]{2,1,0:T(8,128)(2,1)S(1)}, u32[]{:S(2)}) copy-start(bf16[64,112,64]{2,1,0:T(8,128)(2,1)S(1)} %reshape.24) | copy-start | bytes 2752516
  202.6 1.0 copy-start.6
  202.7 280.5 %all-gather.5.cloned.1.call-start = ((), (), s32[]{:S(2)}) async-start(), calls=%async_computation.4 | async-start | bytes 8650752 | tf_op jit(solution)/shard_map/all_gather | solution.py:38
  327.5 6.9 %copy-start.1 = (f32[1024,1024]{1,0:T(8,128)S(1)}, f32[1024,1024]{1,0:T(8,128)}, u32[]{:S(2)}) copy-start(f32[1024,1024]{1,0:T(8,128)} %param.9) | copy-start | bytes 12582916
  337.8 239.7 %reduce-scatter.5.cloned.1.call-start = ((), (), s32[]{:S(2)}) async-start(), calls=%async_computation.5 | async-start | bytes 2621440 | tf_op jit(solution)/shard_map/reduce_scatter | solution.py:46
  495.1 5.6 copy-start.3
  518.7 58.8 %copy-start.4 = (f32[1024,128]{0,1:T(8,128)S(1)}, f32[1024,128]{0,1:T(8,128)}, u32[]{:S(2)}) copy-start(f32[1024,128]{0,1:T(8,128)} %reduce-scatter.3.cloned.1.call-done) | copy-start | bytes 1572868
  518.7 58.8 %copy-start.5 = (f32[1024,128]{0,1:T(8,128)S(1)}, f32[1024,128]{0,1:T(8,128)}, u32[]{:S(2)}) copy-start(f32[1024,128]{0,1:T(8,128)} %get-tuple-element.23) | copy-start | bytes 1572868
Sparse Core Ops, SparseCore 0:
  16.0 151.3 all-gather.2
  202.8 58.5 reduce-scatter.2
  337.9 145.2 all-gather.4
  518.8 58.6 reduce-scatter.4
where the time goes:
time: 655 us; the launch traced here: 653 us
  waiting for transfers between devices  411 us (63%)
  blocking collectives  130 us (20%)
  local copies, waits for them, and re-layouts  44.6 us (7%)
  other arithmetic  27.8 us (4%)
  matrix products  26.7 us (4%)
  between operations  13.9 us (2%)
    all_gather x2, waiting for transfers between devices, per_device(): lax.all_gather(smoothed.astype(jnp.bfloat16), 'col', axis=0, tiled=True)  294 us
    psum x2, blocking collectives, per_device(): gamma_now = lax.psum(local_energy, ('row', 'col'))  130 us
    reduce_scatter x2, waiting for transfers between devices, per_device(): lax.psum_scatter(partial_value.reshape(tile_rows * block_size, rhs_count)...  116 us
    scatter-add x2, other arithmetic, per_device(): jax.ops.segment_sum(products, slot_rows, num_segments=tile_rows, indices_...  23.8 us
    all_gather x2, local copies, waits for them, and re-layouts, per_device(): lax.all_gather(smoothed.astype(jnp.bfloat16), 'col', axis=0, tiled=True)  23.8 us
  transfers between devices with their start and end apart: 4, of which 4 were waited for; matrix products, arithmetic and copies ran while one was open for 0% of the time, Pallas kernels for 0%

commit v1 on v0

--- a/solution.py
+++ b/solution.py
@@ -34,7 +34,7 @@
             preferred_element_type=jnp.float32,
         )
         local_energy = jnp.sum(residual * smoothed, axis=0)
-        gamma_now = lax.psum(local_energy, ("row", "col"))
+        gamma_now = jnp.sum(lax.all_gather(local_energy, ("row", "col")), axis=0)
         gathered = lax.all_gather(smoothed.astype(jnp.bfloat16), "col", axis=0, tiled=True)
         pieces = gathered.reshape(tile_cols, block_size, rhs_count)[block_cols]
         products = jnp.einsum(

time: 655 us -> 1280 us (1.95)
  blocking collectives: 130 us -> 751 us
    all_gather x0 -> x2, blocking collectives: none -> 550 us  [per_device(): gamma_now = jnp.sum(lax.all_gather(local_energy, ('row', 'col')), axis=0)]
    psum x2, blocking collectives: 130 us -> 201 us  [per_device(): delta_now = lax.psum(jnp.sum(smoothed * applied, axis=0), ('row', 'col'))]
where the time goes in v1:
time: 1280 us; the launch traced here: 1270 us
  blocking collectives  751 us (59%)
  waiting for transfers between devices  410 us (32%)
  local copies, waits for them, and re-layouts  44.6 us (3%)
  other arithmetic  28.1 us (2%)
  matrix products  26.6 us (2%)
  between operations  13.9 us (1%)
    all_gather x2, blocking collectives, per_device(): gamma_now = jnp.sum(lax.all_gather(local_energy, ('row', 'col')), axis=0)  550 us
    all_gather x2, waiting for transfers between devices, per_device(): lax.all_gather(smoothed.astype(jnp.bfloat16), 'col', axis=0, tiled=True)  294 us
    psum x2, blocking collectives, per_device(): delta_now = lax.psum(jnp.sum(smoothed * applied, axis=0), ('row', 'col'))  201 us
    reduce_scatter x2, waiting for transfers between devices, per_device(): lax.psum_scatter(partial_value.reshape(tile_rows * block_size, rhs_count)...  116 us
  transfers between devices with their start and end apart: 4, of which 4 were waited for; matrix products, arithmetic and copies ran while one was open for 0% of the time, Pallas kernels for 0%

profile of v1, /device:TPU:1, one launch (start us, length us, event | category | flops | bytes accessed | tf_op | source)
XLA Modules:
  0.0 1274.1 jit_solution(1958612605905980935)
XLA Ops:
  7.2 0.0 all-gather.7.cloned.1.call-start
  7.2 0.0 copy-start
  7.2 5.4 fusion.5
  12.7 0.0 copy-done
  12.7 3.1 fusion.3
  15.8 0.0 all-gather.7.cloned.1.call-update
  15.9 0.0 reduce-scatter.3.cloned.1.call-start
  15.9 2.3 reshape.28
  18.2 0.0 copy-done.7
  18.2 0.1 slice.3
  18.3 0.1 convert_reduce_fusion
  18.4 149.0 %all-gather.7.cloned.1.call-done = bf16[32768,128]{0,1:T(8,128)(2,1)} async-done(((bf16[1024,128]{0,1:T(8,128)(2,1)}), bf16[32768,128]{0,1:T(8,128)(2,1)}) %all-gather.7.cloned.1.call-update) | async-done | bytes 8388624 | tf_op jit(solution)/shard_map/all_gather | solution.py:38
  167.3 11.9 copy.36
  179.2 5.4 gather_fusion
  184.6 3.9 convolution_bitcast_fusion.1
  188.6 0.2 broadcast.12.clone
  188.8 11.9 scatter_fusion
  200.7 1.9 copy.38
  202.6 0.0 reduce-scatter.3.cloned.1.call-update
  202.6 0.0 all-gather.9.cloned.1.call-start
  202.7 1.0 copy-done.6
  203.6 0.2 copy.35
  203.8 57.5 %reduce-scatter.3.cloned.1.call-done = f32[1024,128]{0,1:T(8,128)} async-done(((f32[4096,128]{0,1:T(8,128)}), f32[1024,128]{0,1:T(8,128)}) %reduce-scatter.3.cloned.1.call-update) | async-done | bytes 524304 | tf_op jit(solution)/shard_map/reduce_scatter | solution.py:46
  261.4 1.2 multiply_reduce_fusion.2
  262.6 274.8 %all-gather.2 = f32[128,1,128]{2,1,0:T(1,128)S(1)} all-gather(f32[1,1,128]{2,1,0:T(1,128)S(1)} %bitcast.27), channel_id=2, replica_groups=mesh['row'=4,'col'=32] {'row','col'}, dimensions={0}, use_global_device_ids=true | all-gather | bytes 66048 | tf_op jit(solution)/shard_map/all_gather | solution.py:37
  537.4 100.6 %psum.14 = f32[128]{0:T(128)S(1)} all-reduce(f32[128]{0:T(128)S(1)} %get-tuple-element.12), channel_id=1, replica_groups=mesh['row'=4,'col'=32] {'row','col'}, use_global_device_ids=true, to_apply=%region_6.0 | all-reduce | flops 128 | bytes 1024 | tf_op jit(solution)/shard_map/psum | solution.py:52
  638.0 0.2 reduce_sum.64
  638.2 6.9 fusion.2
  645.1 3.3 fusion.4
  648.4 0.0 all-gather.9.cloned.1.call-update
  648.4 0.0 reduce-scatter.5.cloned.1.call-start
  648.5 144.6 %all-gather.9.cloned.1.call-done = bf16[32768,128]{0,1:T(8,128)(2,1)} async-done(((bf16[1024,128]{0,1:T(8,128)(2,1)}), bf16[32768,128]{0,1:T(8,128)(2,1)}) %all-gather.9.cloned.1.call-update) | async-done | bytes 8388624 | tf_op jit(solution)/shard_map/all_gather | solution.py:38
  793.1 11.9 copy.40
  805.1 5.6 gather_fusion.1
  810.7 3.9 convolution_bitcast_fusion
  814.6 0.2 broadcast.12
  814.9 11.9 scatter_fusion.1
  826.8 1.9 copy.42
  828.6 0.0 reduce-scatter.5.cloned.1.call-update
  828.7 58.8 %reduce-scatter.5.cloned.1.call-done = f32[1024,128]{0,1:T(8,128)} async-done(((f32[4096,128]{0,1:T(8,128)}), f32[1024,128]{0,1:T(8,128)}) %reduce-scatter.5.cloned.1.call-update) | async-done | bytes 524304 | tf_op jit(solution)/shard_map/reduce_scatter | solution.py:46
  887.4 0.0 copy-done.5
  887.4 1.3 multiply_reduce_fusion
  888.7 274.9 %all-gather.3 = f32[128,1,128]{2,1,0:T(1,128)S(1)} all-gather(f32[1,1,128]{2,1,0:T(1,128)S(1)} %bitcast.28), channel_id=3, replica_groups=mesh['row'=4,'col'=32] {'row','col'}, dimensions={0}, use_global_device_ids=true | all-gather | bytes 66048 | tf_op jit(solution)/shard_map/all_gather | solution.py:37
  1163.6 100.4 %psum.15 = f32[128]{0:T(128)S(1)} all-reduce(f32[128]{0:T(128)S(1)} %get-tuple-element.10), channel_id=1, replica_groups=mesh['row'=4,'col'=32] {'row','col'}, use_global_device_ids=true, to_apply=%region_12.0 | all-reduce | flops 128 | bytes 1024 | tf_op jit(solution)/shard_map/psum | solution.py:52
  1264.0 0.2 reduce_sum.68
  1264.1 1.4 multiply_subtract_fusion
  1265.6 1.0 copy.43
  1266.6 1.0 copy.44
  (17 shorter events, 0.1 us)
Async XLA Ops:
  7.2 160.2 %all-gather.7.cloned.1.call-start = ((), (), s32[]{:S(2)}) async-start(), calls=%async_computation.2 | async-start | bytes 8650752 | tf_op jit(solution)/shard_map/all_gather | solution.py:38
  7.2 5.5 copy-start
  15.8 2.4 copy-start.7
  15.8 2.4 copy-start.8
  15.9 245.5 %reduce-scatter.3.cloned.1.call-start = ((), (), s32[]{:S(2)}) async-start(), calls=%async_computation.3 | async-start | bytes 2621440 | tf_op jit(solution)/shard_map/reduce_scatter | solution.py:46
  18.2 166.5 %copy-start.2 = (bf16[64,112,64]{2,1,0:T(8,128)(2,1)}, bf16[64,112,64]{2,1,0:T(8,128)(2,1)S(1)}, u32[]{:S(2)}) copy-start(bf16[64,112,64]{2,1,0:T(8,128)(2,1)S(1)} %reshape.28) | copy-start | bytes 2752516
  202.6 1.0 copy-start.6
  202.6 590.5 %all-gather.9.cloned.1.call-start = ((), (), s32[]{:S(2)}) async-start(), calls=%async_computation.4 | async-start | bytes 8650752 | tf_op jit(solution)/shard_map/all_gather | solution.py:38
  638.2 6.9 copy-start.1
  648.4 239.0 %reduce-scatter.5.cloned.1.call-start = ((), (), s32[]{:S(2)}) async-start(), calls=%async_computation.5 | async-start | bytes 2621440 | tf_op jit(solution)/shard_map/reduce_scatter | solution.py:46
  805.1 5.6 copy-start.3
  828.6 58.8 %copy-start.4 = (f32[1024,128]{0,1:T(8,128)S(1)}, f32[1024,128]{0,1:T(8,128)}, u32[]{:S(2)}) copy-start(f32[1024,128]{0,1:T(8,128)} %reduce-scatter.3.cloned.1.call-done) | copy-start | bytes 1572868
  828.6 58.8 %copy-start.5 = (f32[1024,128]{0,1:T(8,128)S(1)}, f32[1024,128]{0,1:T(8,128)}, u32[]{:S(2)}) copy-start(f32[1024,128]{0,1:T(8,128)} %get-tuple-element.21) | copy-start | bytes 1572868
Sparse Core Ops, SparseCore 0:
  16.0 151.3 all-gather.6
  202.7 58.5 reduce-scatter.2
  648.6 144.5 all-gather.8
  828.8 58.5 reduce-scatter.4
